TPU v7x, 128 devices: a whole 4x4x4 slice. The times are simulated.
128 devices in a mesh: dp: 128 (over x, y, z, core).
Axes of the slice: x: 4, y: 4, z: 4, core: 2. Of those that a mesh axis runs over, the one named last changes fastest.
Arguments:
- hidden_in: bfloat16 [131072, 1024], P('dp'), may hold values from -15 to 15
- lengths: int32 [128, 8], P('dp'), may hold values from 1 to 512, 1024 in all within a row
- owner: int32 [1024], P('dp'), may hold values from 0 to 1023, each once
- pooled_grad: float32 [1024, 1024], P('dp'), may hold values from -6 to 6
- norm_gain: bfloat16 [1024], replicated, may hold values from 0.25 to 1.75
- w_query: bfloat16 [1024, 2048], replicated
- w_key: bfloat16 [1024, 1024], P('dp')
- value_weight: bfloat16 [1024, 1024], P('dp'), may hold values from -0.1875 to 0.1875
- w_out: bfloat16 [2048, 1024], replicated, may hold values from -0.125 to 0.125
Outputs:
- grad_in: bfloat16 [131072, 1024], P('dp')
- grad_key: float32 [1024, 1024], P('dp')
- grad_value: float32 [1024, 1024], P('dp')
- grad_gain: float32 [1024], replicated
Inputs may be any that keep to these rules, and one draw needn't show every extreme that they name: Each row of lengths sums to 1024, and some statement has exactly 512 tokens. `owner`: a permutation.
All inputs are finite; a program needn't handle non-finite values.
Results may differ from a plain program's by a relative error of at most 0.035.
The roundings to bfloat16 on the way count: a program that leaves them out, or rounds other values in their place, can miss the bound.
Values may be sent and summed in bfloat16 or wider, within the bound.
A program may use at most 128 MiB of HBM per device.

v0:
```python
import jax
import jax.numpy as jnp
from jax import lax
from jax.sharding import PartitionSpec as P

QUERY_HEADS = 16
KEY_HEADS = 8
HEAD_WIDTH = 128


def per_device(
    hidden_in, lengths, owner, pooled_grad, norm_gain, w_query, w_key, value_weight, w_out
):
    token_rows = hidden_in.shape[0]
    statement_slots = lengths.shape[1]
    key_value_width = w_key.shape[1]
    head_groups = QUERY_HEADS // KEY_HEADS
    scale_q = 1.0 / HEAD_WIDTH**0.5
    every_grad = lax.all_gather(pooled_grad.astype(jnp.bfloat16), "dp", axis=0, tiled=True).astype(
        pooled_grad.dtype
    )
    cached = jnp.take(every_grad, owner, axis=0)
    inputs_f = hidden_in.astype(jnp.float32)
    inv_rms = lax.rsqrt(jnp.mean(inputs_f * inputs_f, axis=-1, keepdims=True) + 1e-06)
    normed = inputs_f * inv_rms
    normed_b = (normed * norm_gain.astype(jnp.float32)).astype(jnp.bfloat16)
    kv_rows = jnp.concatenate([w_key, value_weight], axis=1)
    kv_full = lax.all_gather(kv_rows, "dp", axis=0, tiled=True)
    key_value_joint = jnp.dot(normed_b, kv_full, preferred_element_type=jnp.float32)
    key_value_joint = key_value_joint.astype(jnp.bfloat16)
    key_rows = key_value_joint[:, :key_value_width].reshape(token_rows, KEY_HEADS, HEAD_WIDTH)
    value_rows = key_value_joint[:, key_value_width:].reshape(token_rows, KEY_HEADS, HEAD_WIDTH)
    ends = jnp.cumsum(lengths[0])
    last_rows = ends - 1
    positions = jnp.arange(token_rows, dtype=jnp.int32)
    segment = jnp.sum((positions[:, None] >= ends[None, :]).astype(jnp.int32), axis=1)
    member = segment[None, :] == jnp.arange(statement_slots, dtype=jnp.int32)[:, None]
    last_normed = jnp.take(normed_b, last_rows, axis=0)
    query_rows = jnp.dot(last_normed, w_query, preferred_element_type=jnp.float32).astype(
        jnp.bfloat16
    )
    query_rows = query_rows.reshape(statement_slots, KEY_HEADS, head_groups, HEAD_WIDTH)
    scores = (
        jnp.einsum("sgqe,tge->sgqt", query_rows, key_rows, preferred_element_type=jnp.float32)
        * scale_q
    )
    scores = jnp.where(member[:, None, None, :], scores, -1e30)
    top = jnp.max(scores, axis=-1, keepdims=True)
    expo = jnp.exp(scores - top)
    probs = expo / jnp.sum(expo, axis=-1, keepdims=True)
    probs_b = probs.astype(jnp.bfloat16)
    attended = jnp.einsum(
        "sgqt,tge->sgqe", probs_b, value_rows, preferred_element_type=jnp.float32
    ).astype(jnp.bfloat16)
    attended = attended.reshape(statement_slots, QUERY_HEADS * HEAD_WIDTH)
    pooled = jnp.take(inputs_f, last_rows, axis=0) + jnp.dot(
        attended, w_out, preferred_element_type=jnp.float32
    )
    inv_len = lax.rsqrt(jnp.sum(pooled * pooled, axis=-1, keepdims=True) + 1e-06)
    embed = pooled * inv_len
    grad_pool = inv_len * (cached - embed * jnp.sum(embed * cached, axis=-1, keepdims=True))
    grad_pool_b = grad_pool.astype(jnp.bfloat16)
    attention_gradient = lax.dot_general(
        grad_pool_b, w_out, (((1,), (1,)), ((), ())), preferred_element_type=jnp.float32
    )
    attention_gradient = attention_gradient.astype(jnp.bfloat16).reshape(
        statement_slots, KEY_HEADS, head_groups, HEAD_WIDTH
    )
    grad_values = jnp.einsum(
        "sgqt,sgqe->tge", probs_b, attention_gradient, preferred_element_type=jnp.float32
    )
    grad_values = grad_values.astype(jnp.bfloat16).reshape(token_rows, key_value_width)
    grad_prob = jnp.einsum(
        "sgqe,tge->sgqt", attention_gradient, value_rows, preferred_element_type=jnp.float32
    )
    grad_score = probs * (grad_prob - jnp.sum(probs * grad_prob, axis=-1, keepdims=True)) * scale_q
    grad_score = grad_score.astype(jnp.bfloat16)
    grad_query = jnp.einsum(
        "sgqt,tge->sgqe", grad_score, key_rows, preferred_element_type=jnp.float32
    )
    grad_query = grad_query.astype(jnp.bfloat16).reshape(statement_slots, QUERY_HEADS * HEAD_WIDTH)
    grad_keys = jnp.einsum(
        "sgqt,sgqe->tge", grad_score, query_rows, preferred_element_type=jnp.float32
    )
    grad_keys = grad_keys.astype(jnp.bfloat16).reshape(token_rows, key_value_width)
    grad_both = jnp.concatenate([grad_keys, grad_values], axis=1)
    grad_normed = lax.dot_general(
        grad_both, kv_full, (((1,), (1,)), ((), ())), preferred_element_type=jnp.float32
    )
    query_back = lax.dot_general(
        grad_query, w_query, (((1,), (1,)), ((), ())), preferred_element_type=jnp.float32
    )
    grad_normed = grad_normed.at[last_rows].add(query_back)
    gain_total = lax.psum(jnp.sum(grad_normed * normed, axis=0), "dp")
    scaled = grad_normed * norm_gain.astype(jnp.float32)
    grad_in = inv_rms * (scaled - normed * jnp.mean(scaled * normed, axis=-1, keepdims=True))
    grad_in = grad_in.at[last_rows].add(grad_pool).astype(jnp.bfloat16)
    weight_share = lax.psum_scatter(
        lax.dot_general(
            normed_b, grad_both, (((0,), (0,)), ((), ())), preferred_element_type=jnp.float32
        ),
        "dp",
        scatter_dimension=0,
        tiled=True,
    )
    return (
        grad_in,
        weight_share[:, :key_value_width],
        weight_share[:, key_value_width:],
        gain_total,
    )


def solution(mesh):
    return jax.shard_map(
        per_device,
        mesh=mesh,
        in_specs=(
            P("dp", None),
            P("dp", None),
            P("dp"),
            P("dp", None),
            P(),
            P(),
            P("dp", None),
            P("dp", None),
            P(),
        ),
        out_specs=(P("dp", None), P("dp", None), P("dp", None), P()),
        check_vma=False,
    )
```

profile of v0, /device:TPU:0, one launch (start us, length us, event | category | flops | bytes accessed | tf_op | source)
XLA Modules:
  0.0 839.9 jit_solution(15867571985289667130)
XLA Ops:
  7.2 0.0 copy-start
  7.2 0.0 copy-start.5
  7.2 0.0 all-gather.5.cloned.1.call-start
  7.2 1.5 convert_element_type.73
  8.7 0.0 all-gather.5.cloned.1.call-update
  8.8 0.0 all-gather.3.cloned.1.call-start
  8.8 1.4 pad_maximum_fusion.3
  10.2 0.0 all-gather.3.cloned.1.call-update
  10.2 0.0 reduce-scatter.2.cloned.1.call-start
  10.2 0.7 convert_element_type.65
  10.9 4.0 convert_element_type.64
  14.9 0.0 copy-start.6
  14.9 0.0 copy-done.5
  14.9 0.2 reduce-window.4
  15.1 0.0 copy-done
  15.1 0.5 multiply_reduce_fusion.2
  15.6 1.9 multiply_convert_fusion
  17.5 2.4 gather_fusion
  19.9 2.8 gather_fusion.1
  22.7 0.0 copy-done.6
  22.8 0.1 convert_reduce_fusion
  22.9 2.9 convolution_convert_fusion.2
  25.8 53.7 %all-gather.5.cloned.1.call-done = bf16[1024,1024]{1,0:T(8,128)(2,1)} async-done(((bf16[8,1024]{1,0:T(8,128)(2,1)}), bf16[1024,1024]{1,0:T(8,128)(2,1)}) %all-gather.5.cloned.1.call-update) | async-done | bytes 2097168 | tf_op jit(solution)/shard_map/all_gather | solution.py:19
  79.5 4.0 convert_element_type.74
  83.5 2.8 gather_fusion.2
  86.3 61.3 %all-gather.3.cloned.1.call-done = bf16[1024,2048]{1,0:T(8,128)(2,1)} async-done(((bf16[8,2048]{1,0:T(8,128)(2,1)}), bf16[1024,2048]{1,0:T(8,128)(2,1)}) %all-gather.3.cloned.1.call-update) | async-done | bytes 4194320 | tf_op jit(solution)/shard_map/all_gather | solution.py:28
  147.6 7.3 convolution_convert_fusion
  154.9 1.2 slice_bitcast_fusion.1
  156.1 2.0 copy.35
  158.1 2.0 copy.36
  160.1 2.4 fusion.58
  162.5 0.0 copy-start.2
  162.5 2.3 fusion.33
  164.8 0.5 copy-done.2
  165.3 0.0 copy-start.4
  165.3 0.8 multiply_reduce_fusion.5
  166.1 0.2 multiply_reduce_fusion.4
  166.3 1.2 convolution_convert_fusion.1
  167.5 0.0 copy-done.4
  167.5 0.7 fusion.13
  168.2 2.1 bitcast_convert_fusion
  170.3 2.8 bitcast_convert_fusion.1
  173.1 10.6 %fusion.2 = f32[1024,2048]{1,0:T(8,128)} fusion(bf16[1024,1024]{1,0:T(8,128)(2,1)} %multiply_convert_fusion, bf16[1024,1024]{0,1:T(8,128)(2,1)} %bitcast.63, bf16[1024,1024]{0,1:T(8,128)(2,1)} %bitcast.75), kind=kOutput, calls=%fused_computation.16 | convolution fusion | flops 4303355904 | bytes 14680064 | tf_op jit(solution)/shard_map/dot_general | solution.py:99
  183.7 0.0 reduce-scatter.2.cloned.1.call-update
  183.7 2.4 fusion.30
  186.1 0.0 copy-start.3
  186.1 0.0 copy-start.7
  186.1 3.5 fusion.61
  189.6 0.0 copy-done.3
  189.6 0.0 copy-done.7
  189.6 8.4 %fusion.3 = f32[1024,1024]{1,0:T(8,128)} fusion(bf16[1024,2048]{1,0:T(8,128)(2,1)} %all-gather.3.cloned.1.call-done, bf16[1024,1024]{0,1:T(8,128)(2,1)S(1)} %bitcast.64, bf16[1024,1024]{0,1:T(8,128)(2,1)S(1)} %bitcast.76), kind=kOutput, calls=%fused_computation.17 | convolution fusion | flops 4303355904 | bytes 12582912 | tf_op jit(solution)/shard_map/dot_general | solution.py:87
  198.1 4.8 scatter_fusion
  202.8 0.0 copy-start.1
  202.8 3.5 multiply_reduce_fusion
  206.3 0.0 copy-done.1
  206.3 2.9 subtract_multiply_fusion
  209.3 4.9 scatter_custom_fusion.1
  214.1 3.8 convert_element_type.84
  218.0 64.0 %psum.7 = f32[1024]{0:T(1024)} all-reduce(f32[1024]{0:T(1024)S(1)} %get-tuple-element.5), channel_id=1, replica_groups=mesh['dp'=128] {'dp'}, use_global_device_ids=true, to_apply=%region_13.15 | all-reduce | flops 1024 | bytes 8192 | tf_op jit(solution)/shard_map/psum | solution.py:94
  282.0 550.0 %reduce-scatter.2.cloned.1.call-done = f32[8,2048]{1,0:T(8,128)} async-done(((f32[1024,2048]{1,0:T(8,128)}), f32[8,2048]{1,0:T(8,128)}) %reduce-scatter.2.cloned.1.call-update) | async-done | bytes 65552 | tf_op jit(solution)/shard_map/reduce_scatter | solution.py:98
  831.9 1.4 fusion.57
  (11 shorter events, 0.1 us)
Async XLA Ops:
  7.2 7.9 copy-start
  7.2 7.7 copy-start.5
  7.2 72.3 %all-gather.5.cloned.1.call-start = ((), (), s32[]{:S(2)}) async-start(), calls=%async_computation.2 | async-start | bytes 2113536 | tf_op jit(solution)/shard_map/all_gather | solution.py:19
  8.8 138.8 %all-gather.3.cloned.1.call-start = ((), (), s32[]{:S(2)}) async-start(), calls=%async_computation.1 | async-start | bytes 4227072 | tf_op jit(solution)/shard_map/all_gather | solution.py:28
  10.2 821.8 %reduce-scatter.2.cloned.1.call-start = ((), (), s32[]{:S(2)}) async-start(), calls=%async_computation.3 | async-start | bytes 8454144 | tf_op jit(solution)/shard_map/reduce_scatter | solution.py:98
  14.9 7.8 copy-start.6
  162.5 2.8 copy-start.2
  165.3 2.2 copy-start.4
  186.1 3.5 copy-start.3
  186.1 3.5 copy-start.7
  202.8 3.5 copy-start.1
Sparse Core Ops, SparseCore 0:
  11.7 67.7 all-gather.4
  83.2 64.2 all-gather.2
  183.8 648.0 reduce-scatter.1
where the time goes:
time: 841 us; the launch traced here: 840 us
  waiting for transfers between devices  665 us (79%)
  blocking collectives  64 us (8%)
  matrix products  47.4 us (6%)
  other arithmetic  34.3 us (4%)
  local copies, waits for them, and re-layouts  15.1 us (2%)
  between operations  13.9 us (2%)
    reduce_scatter x1, waiting for transfers between devices, per_device(): lax.psum_scatter(lax.dot_general(normed_b, grad_both, (((0,), (0,)), ((),...  550 us
    psum x1, blocking collectives, per_device(): gain_total = lax.psum(jnp.sum(grad_normed * normed, axis=0), 'dp')  64 us
    all_gather x1, waiting for transfers between devices, per_device(): kv_full = lax.all_gather(kv_rows, 'dp', axis=0, tiled=True)  61.3 us
    all_gather x1, waiting for transfers between devices, per_device(): lax.all_gather(pooled_grad.astype(jnp.bfloat16), 'dp', axis=0, tiled=True)  53.7 us
  transfers between devices with their start and end apart: 3, of which 3 were waited for; matrix products, arithmetic and copies ran while one was open for 7% of the time, Pallas kernels for 0%

commit v1 on v0

--- a/solution.py
+++ b/solution.py
@@ -16,9 +16,12 @@
     key_value_width = w_key.shape[1]
     head_groups = QUERY_HEADS // KEY_HEADS
     scale_q = 1.0 / HEAD_WIDTH**0.5
-    every_grad = lax.all_gather(pooled_grad.astype(jnp.bfloat16), "dp", axis=0, tiled=True).astype(
-        pooled_grad.dtype
-    )
+    every_grad = jnp.concatenate(
+        lax.all_to_all(
+            jnp.stack([pooled_grad.astype(jnp.bfloat16)] * lax.axis_size("dp")), "dp", 0, 0
+        ),
+        axis=0,
+    ).astype(pooled_grad.dtype)
     cached = jnp.take(every_grad, owner, axis=0)
     inputs_f = hidden_in.astype(jnp.float32)
     inv_rms = lax.rsqrt(jnp.mean(inputs_f * inputs_f, axis=-1, keepdims=True) + 1e-06)

time: 841 us -> 789 us (0.938)
  waiting for transfers between devices: 665 us -> 603 us
  starting transfers between devices: 0.12 us -> 11.8 us
    all_gather x1 -> x0, waiting for transfers between devices: 53.7 us -> none  [per_device(): lax.all_gather(pooled_grad.astype(jnp.bfloat16), 'dp', axis=0, tiled=True)]
    all_gather x1, waiting for transfers between devices: 61.3 us -> 35.4 us  [per_device(): kv_full = lax.all_gather(kv_rows, 'dp', axis=0, tiled=True)]
    all_to_all x0 -> x1, waiting for transfers between devices: none -> 17 us  [per_device(): lax.all_to_all(jnp.stack([pooled_grad.astype(jnp.bfloat16)] * lax.axis_si...]
    all_to_all x0 -> x1, starting transfers between devices: none -> 11.7 us  [per_device(): lax.all_to_all(jnp.stack([pooled_grad.astype(jnp.bfloat16)] * lax.axis_si...]
where the time goes in v1:
time: 789 us
  waiting for transfers between devices  603 us (76%)
  blocking collectives  64.1 us (8%)
  matrix products  47.4 us (6%)
  other arithmetic  31.5 us (4%)
  local copies, waits for them, and re-layouts  16.7 us (2%)
  between operations  14.2 us (2%)
  starting transfers between devices  11.8 us (1%)
    reduce_scatter x1, waiting for transfers between devices, per_device(): lax.psum_scatter(lax.dot_general(normed_b, grad_both, (((0,), (0,)), ((),...  551 us
    psum x1, blocking collectives, per_device(): gain_total = lax.psum(jnp.sum(grad_normed * normed, axis=0), 'dp')  64.1 us
    all_gather x1, waiting for transfers between devices, per_device(): kv_full = lax.all_gather(kv_rows, 'dp', axis=0, tiled=True)  35.4 us
    all_to_all x1, waiting for transfers between devices, per_device(): lax.all_to_all(jnp.stack([pooled_grad.astype(jnp.bfloat16)] * lax.axis_si...  17 us
  transfers between devices with their start and end apart: 3, of which 3 were waited for; matrix products, arithmetic and copies ran while one was open for 7% of the time, Pallas kernels for 0%

profile of v1, /device:TPU:0, one launch (start us, length us, event | category | flops | bytes accessed | tf_op | source)
XLA Modules:
  0.0 788.6 jit_solution(6064195615085665747)
XLA Ops:
  7.2 0.0 copy-start.5
  7.2 0.0 copy-start
  7.2 0.0 all-gather.2.cloned.1.call-start
  7.2 1.5 pad_maximum_fusion.3
  8.7 0.0 all-gather.2.cloned.1.call-update
  8.7 0.8 convert_element_type.76
  9.5 1.6 stack.2
  11.1 11.7 %all-to-all-start = ((bf16[128,8,1024]{2,1,0:T(8,128)(2,1)}), bf16[128,8,1024]{2,1,0:T(8,128)(2,1)}, u32[]{:S(2)}, u32[]{:S(2)}) async-start(bf16[128,8,1024]{2,1,0:T(8,128)(2,1)} %stack.2), calls=%async_computation | async-start | bytes 4194304 | tf_op jit(solution)/shard_map/all_to_all | solution.py:20
  22.8 0.0 copy-start.6
  22.8 0.0 reduce-scatter.2.cloned.1.call-start
  22.8 0.0 copy-done.5
  22.9 0.0 copy-done
  22.9 2.5 convert_element_type.67
  25.4 0.0 copy-start.7
  25.4 0.0 copy-done.6
  25.4 0.2 reduce-window.4
  25.6 0.5 multiply_reduce_fusion.2
  26.1 1.9 multiply_convert_fusion
  28.0 2.4 gather_fusion
  30.5 2.8 gather_fusion.1
  33.2 0.0 copy-done.7
  33.3 0.1 convert_reduce_fusion
  33.4 2.9 convolution_convert_fusion.2
  36.3 17.0 %all-to-all-done = bf16[128,8,1024]{2,1,0:T(8,128)(2,1)} async-done(((bf16[128,8,1024]{2,1,0:T(8,128)(2,1)}), bf16[128,8,1024]{2,1,0:T(8,128)(2,1)}, u32[]{:S(2)}, u32[]{:S(2)}) %all-to-all-start) | async-done | bytes 2097184 | tf_op jit(solution)/shard_map/all_to_all | solution.py:20
  53.2 4.1 bitcast_convert_fusion.2
  57.3 2.8 gather_fusion.2
  60.1 35.4 %all-gather.2.cloned.1.call-done = bf16[1024,2048]{1,0:T(8,128)(2,1)} async-done(((bf16[8,2048]{1,0:T(8,128)(2,1)}), bf16[1024,2048]{1,0:T(8,128)(2,1)}) %all-gather.2.cloned.1.call-update) | async-done | bytes 4194320 | tf_op jit(solution)/shard_map/all_gather | solution.py:31
  95.5 7.3 convolution_convert_fusion
  102.8 1.2 slice_bitcast_fusion.1
  104.0 2.0 copy.35
  106.0 1.9 copy.36
  107.9 2.4 fusion.58
  110.4 0.0 copy-start.2
  110.4 2.3 fusion.33
  112.6 0.5 copy-done.2
  113.2 0.0 copy-start.4
  113.2 0.8 multiply_reduce_fusion.5
  114.0 0.2 multiply_reduce_fusion.4
  114.2 1.2 convolution_convert_fusion.1
  115.4 0.0 copy-done.4
  115.4 0.7 fusion.13
  116.0 2.1 bitcast_convert_fusion
  118.1 2.8 bitcast_convert_fusion.1
  120.9 10.7 %fusion.2 = f32[1024,2048]{1,0:T(8,128)} fusion(bf16[1024,1024]{1,0:T(8,128)(2,1)} %multiply_convert_fusion, bf16[1024,1024]{0,1:T(8,128)(2,1)} %bitcast.66, bf16[1024,1024]{0,1:T(8,128)(2,1)} %bitcast.78), kind=kOutput, calls=%fused_computation.16 | convolution fusion | flops 4303355904 | bytes 14680064 | tf_op jit(solution)/shard_map/dot_general | solution.py:102
  131.6 0.0 reduce-scatter.2.cloned.1.call-update
  131.6 2.4 fusion.30
  134.0 0.0 copy-start.3
  134.0 0.0 copy-start.8
  134.0 3.5 fusion.61
  137.5 0.0 copy-done.3
  137.5 0.0 copy-done.8
  137.5 8.4 %fusion.3 = f32[1024,1024]{1,0:T(8,128)} fusion(bf16[1024,2048]{1,0:T(8,128)(2,1)} %all-gather.2.cloned.1.call-done, bf16[1024,1024]{0,1:T(8,128)(2,1)S(1)} %bitcast.67, bf16[1024,1024]{0,1:T(8,128)(2,1)S(1)} %bitcast.79), kind=kOutput, calls=%fused_computation.17 | convolution fusion | flops 4303355904 | bytes 12582912 | tf_op jit(solution)/shard_map/dot_general | solution.py:90
  145.9 4.8 scatter_fusion
  150.7 0.0 copy-start.1
  150.7 3.5 multiply_reduce_fusion
  154.2 0.0 copy-done.1
  154.2 2.9 subtract_multiply_fusion
  157.1 4.8 scatter_custom_fusion.1
  161.9 3.8 convert_element_type.88
  165.7 64.1 %psum.7 = f32[1024]{0:T(1024)} all-reduce(f32[1024]{0:T(1024)S(1)} %get-tuple-element.5), channel_id=1, replica_groups=mesh['dp'=128] {'dp'}, use_global_device_ids=true, to_apply=%region_13.15 | all-reduce | flops 1024 | bytes 8192 | tf_op jit(solution)/shard_map/psum | solution.py:97
  229.8 550.5 %reduce-scatter.2.cloned.1.call-done = f32[8,2048]{1,0:T(8,128)} async-done(((f32[1024,2048]{1,0:T(8,128)}), f32[8,2048]{1,0:T(8,128)}) %reduce-scatter.2.cloned.1.call-update) | async-done | bytes 65552 | tf_op jit(solution)/shard_map/reduce_scatter | solution.py:101
  780.4 1.4 fusion.57
  (12 shorter events, 0.1 us)
Async XLA Ops:
  7.2 15.7 %copy-start.5 = (bf16[1024]{0:T(1024)(128)(2,1)S(1)}, bf16[1024]{0:T(1024)(128)(2,1)}, u32[]{:S(2)}) copy-start(bf16[1024]{0:T(1024)(128)(2,1)} %param.15) | copy-start | bytes 6148
  7.2 15.7 %copy-start = (bf16[1024,1024]{1,0:T(8,128)(2,1)S(1)}, bf16[1024,1024]{1,0:T(8,128)(2,1)}, u32[]{:S(2)}) copy-start(bf16[1024,1024]{1,0:T(8,128)(2,1)} %param.11) | copy-start | bytes 6291460
  7.2 88.3 %all-gather.2.cloned.1.call-start = ((), (), s32[]{:S(2)}) async-start(), calls=%async_computation.2 | async-start | bytes 4227072 | tf_op jit(solution)/shard_map/all_gather | solution.py:31
  11.1 42.1 %all-to-all-start = ((bf16[128,8,1024]{2,1,0:T(8,128)(2,1)}), bf16[128,8,1024]{2,1,0:T(8,128)(2,1)}, u32[]{:S(2)}, u32[]{:S(2)}) async-start(bf16[128,8,1024]{2,1,0:T(8,128)(2,1)} %stack.2), calls=%async_computation | async-start | bytes 4194304 | tf_op jit(solution)/shard_map/all_to_all | solution.py:20
  22.8 2.6 copy-start.6
  22.8 757.6 %reduce-scatter.2.cloned.1.call-start = ((), (), s32[]{:S(2)}) async-start(), calls=%async_computation.3 | async-start | bytes 8454144 | tf_op jit(solution)/shard_map/reduce_scatter | solution.py:101
  25.4 7.9 copy-start.7
  110.4 2.8 copy-start.2
  113.2 2.2 copy-start.4
  134.0 3.5 copy-start.3
  134.0 3.5 copy-start.8
  150.7 3.5 copy-start.1
Sparse Core Ops, SparseCore 0:
  11.8 83.6 all-gather.1
  131.7 648.5 reduce-scatter.1
